TPU v7x, 32 devices: a whole 2x2x4 slice. The times are simulated.
32 devices in a mesh: groups: 2 (over y), ctx: 16 (over z, x, core).
Axes of the slice: x: 2, y: 2, z: 4, core: 2. Of those that a mesh axis runs over, the one named last changes fastest.
Arguments:
- queries: bfloat16 [512, 5120], P(('groups', 'ctx')), parts along dimension 0, may hold values from -45 to 45
- keys: bfloat16 [49152, 1024], P(('groups', 'ctx')), parts along dimension 0, may hold values from -5 to 5
- values: bfloat16 [49152, 1024], P(('groups', 'ctx')), parts along dimension 0, may hold values from -10 to 10
- block_mask: int32 [16, 2, 192], P('groups', None, 'ctx'), parts along dimension 0, may hold values from 0 to 1, as said below
- out_weight: bfloat16 [5120, 5120], P('ctx'), may hold values from -0.078125 to 0.078125
Outputs:
- projected: bfloat16 [512, 5120], P(('groups', 'ctx')), parts along dimension 0
There are 2 independent parts, one for each index of `groups`. A program takes and returns all parts, laid end to end along the dimension named above; an argument that names none is the same for every part. Nothing has to cross between parts.
Inputs may be any that keep to these rules, and one draw needn't show every extreme that they name: `block_mask`: for every key head and query block at least one key block is 1; the share of 1s differs between spans of 1536 positions.
All inputs are finite; a program needn't handle non-finite values.
Results may differ from a plain program's by a relative error of at most 0.0055.
Values may be sent and summed in bfloat16 or wider, within the bound.
A program may use at most 128 MiB of HBM per device.

v0:
```python
import math
import jax
import jax.numpy as jnp
from jax import lax
from jax.sharding import PartitionSpec as P

HEAD_SIZE = 128
NEG = -1e30


def shards(queries, keys, values, block_mask, out_weight):
    whole = lax.all_gather(queries, "ctx", axis=0, tiled=True)
    qtok, width = whole.shape
    kdev = keys.shape[0]
    heads_kv, query_block_count, key_block_count = block_mask.shape
    head_dim = HEAD_SIZE
    query_group = width // head_dim // heads_kv
    scale = 1.0 / math.sqrt(head_dim)
    query_tensor = whole.reshape(qtok, heads_kv, query_group, head_dim)
    key_tensor = keys.reshape(kdev, heads_kv, head_dim)
    value_tensor = values.reshape(kdev, heads_kv, head_dim)

    def head_scores(head):
        q_h = lax.dynamic_index_in_dim(query_tensor, head, 1, keepdims=False)
        k_h = lax.dynamic_index_in_dim(key_tensor, head, 1, keepdims=False)
        scores = jnp.einsum("qge,ke->gqk", q_h, k_h, preferred_element_type=jnp.float32) * scale
        blocks = lax.dynamic_index_in_dim(block_mask, head, 0, keepdims=False)
        live = jnp.broadcast_to(
            blocks[:, None, :, None] > 0,
            (
                query_block_count,
                qtok // query_block_count,
                key_block_count,
                kdev // key_block_count,
            ),
        )
        return (scores, live.reshape(qtok, kdev))

    def max_step(head, maxima):
        scores, live = head_scores(head)
        local = jnp.max(jnp.where(live[None], scores, NEG), axis=2)
        return lax.dynamic_update_slice(maxima, local.T[:, None, :], (0, head, 0))

    maxima = lax.fori_loop(
        0, heads_kv, max_step, jnp.full((qtok, heads_kv, query_group), NEG, jnp.float32)
    )
    row_max = lax.pmax(maxima, "ctx")

    def sum_step(head, carry):
        numer, denom = carry
        scores, live = head_scores(head)
        top = lax.dynamic_index_in_dim(row_max, head, 1, keepdims=False).T[:, :, None]
        probs = jnp.where(live[None], jnp.exp(scores - top), 0.0).astype(jnp.bfloat16)
        total = jnp.sum(probs.astype(jnp.float32), axis=2)
        v_h = lax.dynamic_index_in_dim(value_tensor, head, 1, keepdims=False)
        weighted = jnp.einsum("gqk,ke->qge", probs, v_h, preferred_element_type=jnp.float32)
        numer = lax.dynamic_update_slice(
            numer, weighted.reshape(qtok, 1, query_group * head_dim), (0, head, 0)
        )
        denom = lax.dynamic_update_slice(denom, total.T[:, None, :], (0, head, 0))
        return (numer, denom)

    start_numer = jnp.zeros((qtok, heads_kv, query_group * head_dim), jnp.float32)
    start_denom = jnp.zeros((qtok, heads_kv, query_group), jnp.float32)
    numer, denom = lax.fori_loop(0, heads_kv, sum_step, (start_numer, start_denom))
    numer = numer.reshape(qtok, width)
    denom = denom.reshape(qtok, heads_kv * query_group)
    num_rows, den_rows = (
        lax.psum_scatter(numer, "ctx", scatter_dimension=0, tiled=True),
        lax.psum_scatter(denom, "ctx", scatter_dimension=0, tiled=True),
    )
    own_rows = num_rows.shape[0]
    attn_rows = (num_rows.reshape(own_rows, -1, head_dim) / den_rows[:, :, None]).reshape(
        own_rows, width
    )
    attn_cols = lax.all_to_all(
        attn_rows.astype(jnp.bfloat16), "ctx", split_axis=1, concat_axis=0, tiled=True
    )
    summed = lax.psum_scatter(
        jnp.dot(attn_cols, out_weight, preferred_element_type=jnp.float32),
        "ctx",
        scatter_dimension=0,
        tiled=True,
    )
    return summed.astype(jnp.bfloat16)


def solution(mesh):
    return jax.shard_map(
        shards,
        mesh=mesh,
        in_specs=(
            P(("groups", "ctx"), None),
            P(("groups", "ctx"), None),
            P(("groups", "ctx"), None),
            P("groups", None, "ctx"),
            P("ctx", None),
        ),
        out_specs=P(("groups", "ctx"), None),
        check_vma=False,
    )
```

profile of v0, /device:TPU:0, one launch (start us, length us, event | category | flops | bytes accessed | tf_op | source)
XLA Modules:
  0.0 496.8 jit_solution(2088119072019379952)
XLA Ops:
  7.3 4.9 copy.38
  12.2 4.7 copy.42
  16.9 4.7 copy.37
  21.6 34.0 %all-gather.2.cloned.1.call-done = bf16[256,5120]{1,0:T(8,128)(2,1)} async-done(((bf16[16,5120]{1,0:T(8,128)(2,1)}), bf16[256,5120]{1,0:T(8,128)(2,1)}) %all-gather.2.cloned.1.call-update) | async-done | bytes 2621456 | tf_op jit(solution)/shard_map/all_gather | solution.py:12
  55.6 4.4 copy.39
  60.0 4.3 copy.43
  64.3 53.1 %while.28 = (s32[]{:T(128)}, f32[256,8,5]{0,2,1:T(8,128)S(1)}, s32[8,2,12]{2,1,0:T(2,128)}, bf16[1536,8,128]{2,0,1:T(8,128)(2,1)}, bf16[256,8,5,128]{3,0,2,1:T(8,128)(2,1)}, /*index=5*/s32[]{:T(128)}) while((s32[]{:T(128)}, f32[256,8,5]{0,2,1:T(8,128)S(1)}, s32[8,2,12]{2,1,0:T(2,128)}, bf16[1536,8,128]{2,0,1:T(8,128)(2,1)}, ...), condition=%wide.region_2.3_spmd, body=%wide.region_0.2_spmd.sunk | while | flops 509213472 | bytes 3102949 | solution.py:44
  66.1 2.2 copy.63
  68.4 2.5 fusion.31
  72.8 2.2 copy.63
  75.0 2.5 fusion.31
  79.4 2.2 copy.63
  81.6 2.5 fusion.31
  86.1 2.2 copy.63
  88.3 2.5 fusion.31
  92.7 2.2 copy.63
  94.9 2.5 fusion.31
  99.3 2.2 copy.63
  101.5 2.5 fusion.31
  106.0 2.2 copy.63
  108.2 2.5 fusion.31
  112.6 2.2 copy.63
  114.8 2.5 fusion.31
  117.4 59.4 %pmax.7 = f32[256,8,5]{0,2,1:T(8,128)S(1)} all-reduce(f32[256,8,5]{0,2,1:T(8,128)S(1)} %get-tuple-element.239), channel_id=1, replica_groups=mesh['groups'=2,'ctx'=16] {'ctx'}, use_global_device_ids=true, to_apply=%region_3.4 | all-reduce | flops 10240 | bytes 81920 | tf_op jit(solution)/shard_map/pmax | solution.py:47
  176.8 80.6 %while.29 = (s32[]{:T(128)}, f32[256,8,640]{0,2,1:T(8,128)}, f32[256,8,5]{0,2,1:T(8,128)S(1)}, bf16[1536,8,128]{0,2,1:T(8,128)(2,1)}, s32[8,2,12]{2,1,0:T(2,128)...) while((s32[]{:T(128)}, f32[256,8,640]{0,2,1:T(8,128)}, ...), condition=%wide.region_6.7_spmd, body=%wide.region_4.6_spmd.sunk | while | flops 1018428160 | bytes 13341961 | solution.py:65
  178.7 2.2 copy.65
  180.9 3.4 convert_reduce_fusion.2
  188.7 2.2 copy.65
  190.9 3.4 convert_reduce_fusion.2
  198.8 2.2 copy.65
  201.0 3.4 convert_reduce_fusion.2
  208.9 2.2 copy.65
  211.1 3.4 convert_reduce_fusion.2
  219.0 2.2 copy.65
  221.2 3.4 convert_reduce_fusion.2
  229.1 2.2 copy.65
  231.3 3.4 convert_reduce_fusion.2
  239.1 2.2 copy.65
  241.3 3.4 convert_reduce_fusion.2
  249.2 2.2 copy.65
  251.4 3.4 convert_reduce_fusion.2
  258.3 6.0 %copy.44 = f32[256,5120]{1,0:T(8,128)} copy(f32[256,5120]{0,1:T(8,128)} %bitcast.123) | data formatting | bytes 10485760 | tf_op jit(solution)/shard_map/reshape | solution.py:66
  264.3 46.3 %reduce-scatter.10.cloned.1.call-done = f32[16,40]{1,0:T(8,128)} async-done(((f32[256,40]{1,0:T(8,128)}), f32[16,40]{1,0:T(8,128)}) %reduce-scatter.10.cloned.1.call-update) | async-done | bytes 2576 | tf_op jit(solution)/shard_map/reduce_scatter | solution.py:70
  310.7 81.4 %reduce-scatter.6.cloned.1.call-done = f32[16,5120]{1,0:T(8,128)} async-done(((f32[256,5120]{1,0:T(8,128)}), f32[16,5120]{1,0:T(8,128)}) %reduce-scatter.6.cloned.1.call-update) | async-done | bytes 327696 | tf_op jit(solution)/shard_map/reduce_scatter | solution.py:69
  392.9 1.7 fusion.18
  395.7 12.4 %all_to_all.19 = bf16[16,16,320]{2,0,1:T(8,128)(2,1)S(1)} all-to-all(bf16[16,16,320]{2,0,1:T(8,128)(2,1)S(1)} %copy.46), channel_id=1, replica_groups=mesh['groups'=2,'ctx'=16] {'ctx'}, dimensions={1} | all-to-all | bytes 327680 | tf_op jit(solution)/shard_map/all_to_all | solution.py:76
  408.2 3.9 fusion.19
  412.1 76.6 %reduce-scatter.8.cloned.1.call-done = f32[16,5120]{1,0:T(8,128)} async-done(((f32[256,5120]{1,0:T(8,128)}), f32[16,5120]{1,0:T(8,128)}) %reduce-scatter.8.cloned.1.call-update) | async-done | bytes 327696 | tf_op jit(solution)/shard_map/reduce_scatter | solution.py:79
  (107 shorter events, 55.4 us)
Async XLA Ops:
  6.5 401.6 %copy-start = (bf16[320,5120]{1,0:T(8,128)(2,1)S(1)}, bf16[320,5120]{1,0:T(8,128)(2,1)}, u32[]{:S(2)}) copy-start(bf16[320,5120]{1,0:T(8,128)(2,1)} %param.13) | copy-start | bytes 9830404
  6.5 49.0 %all-gather.2.cloned.1.call-start = ((), (), s32[]{:S(2)}) async-start(), calls=%async_computation.4 | async-start | bytes 2785280 | tf_op jit(solution)/shard_map/all_gather | solution.py:12
  7.3 303.4 %reduce-scatter.10.cloned.1.call-start = ((), (), s32[]{:S(2)}) async-start(), calls=%async_computation.7 | async-start | bytes 139264 | tf_op jit(solution)/shard_map/reduce_scatter | solution.py:70
  258.2 133.8 %reduce-scatter.6.cloned.1.call-start = ((), (), s32[]{:S(2)}) async-start(), calls=%async_computation.5 | async-start | bytes 5570560 | tf_op jit(solution)/shard_map/reduce_scatter | solution.py:69
  264.3 224.4 %reduce-scatter.8.cloned.1.call-start = ((), (), s32[]{:S(2)}) async-start(), calls=%async_computation.6 | async-start | bytes 5570560 | tf_op jit(solution)/shard_map/reduce_scatter | solution.py:79
Sparse Core Ops, SparseCore 0:
  9.6 45.8 all-gather.1
  258.4 52.2 reduce-scatter.9
  314.5 77.4 reduce-scatter.5
  412.2 76.4 reduce-scatter.7
where the time goes:
time: 499 us; the launch traced here: 497 us
  waiting for transfers between devices  239 us (48%)
  local copies, waits for them, and re-layouts  92.9 us (19%)
  blocking collectives  71.9 us (14%)
  matrix products  64.9 us (13%)
  other arithmetic  14.3 us (3%)
  between operations  13.2 us (3%)
    reduce_scatter x1, waiting for transfers between devices, shards(): lax.psum_scatter(numer, 'ctx', scatter_dimension=0, tiled=True)  81.4 us
    reduce_scatter x1, waiting for transfers between devices, shards(): lax.psum_scatter(jnp.dot(attn_cols, out_weight, preferred_element_type=jn...  76.6 us
    pmax x1, blocking collectives, shards(): row_max = lax.pmax(maxima, 'ctx')  59.4 us
    dot_general x16, matrix products, head_scores(): jnp.einsum('qge,ke->gqk', q_h, k_h, preferred_element_type=jnp.float32)  47.6 us
    reduce_scatter x1, waiting for transfers between devices, shards(): lax.psum_scatter(denom, 'ctx', scatter_dimension=0, tiled=True)  46.3 us
    all_gather x1, waiting for transfers between devices, shards(): whole = lax.all_gather(queries, 'ctx', axis=0, tiled=True)  34 us
    broadcast_in_dim x8, local copies, waits for them, and re-layouts, max_step(): local = jnp.max(jnp.where(live[None], scores, NEG), axis=2)  17.8 us
    broadcast_in_dim x8, local copies, waits for them, and re-layouts, sum_step(): jnp.where(live[None], jnp.exp(scores - top), 0.0).astype(jnp.bfloat16)  17.8 us
  transfers between devices with their start and end apart: 4, of which 4 were waited for; matrix products, arithmetic and copies ran while one was open for 4% of the time, Pallas kernels for 0%

commit v1 on v0

--- a/solution.py
+++ b/solution.py
@@ -8,8 +8,30 @@
 NEG = -1e30
 
 
+def laid_out(parts, dim):
+    lengths = list(parts.shape[1:])
+    lengths[dim] *= parts.shape[0]
+    return jnp.moveaxis(parts, 0, dim).reshape(lengths)
+
+
+def ring_gather(x, axis, dim):
+    size = lax.axis_size(axis)
+    pairs = [(i, (i + 1) % size) for i in range(size)]
+    back = [(b, a) for a, b in pairs]
+    lower, upper = ([], [])
+    for lap in range(size - 1):
+        if lap % 2 == 0:
+            lower.append(lax.ppermute(lower[-1] if lower else x, axis, pairs))
+        else:
+            upper.append(lax.ppermute(upper[-1] if upper else x, axis, back))
+    pieces = jnp.stack([*lower[::-1], x, *upper])
+    shift = lax.axis_index(axis) - len(lower)
+    pieces = pieces[(jnp.arange(size) - shift) % size]
+    return laid_out(pieces, dim)
+
+
 def shards(queries, keys, values, block_mask, out_weight):
-    whole = lax.all_gather(queries, "ctx", axis=0, tiled=True)
+    whole = ring_gather(queries, "ctx", 0)
     qtok, width = whole.shape
     kdev = keys.shape[0]
     heads_kv, query_block_count, key_block_count = block_mask.shape

time: 499 us -> 551 us (1.10)
  starting transfers between devices: 0.12 us -> 32.9 us
  local copies, waits for them, and re-layouts: 92.9 us -> 122 us
  waiting for transfers between devices: 239 us -> 230 us
    all_gather x1 -> x0, waiting for transfers between devices: 34 us -> none  [shards(): whole = lax.all_gather(queries, 'ctx', axis=0, tiled=True)]
    ppermute x0 -> x15, starting transfers between devices: none -> 32.8 us  [the longest x7 32.4 us: ring_gather(): upper.append(lax.ppermute(upper[-1] if upper else x, axis, back))]
    ppermute x0 -> x15, waiting for transfers between devices: none -> 25.1 us  [the longest x8 22.1 us: ring_gather(): lower.append(lax.ppermute(lower[-1] if lower else x, axis, pairs))]
    unnamed x5 -> x44, local copies, waits for them, and re-layouts: 10.4 us -> 30.2 us
    another operation x0 -> x2, local copies, waits for them, and re-layouts: none -> 7.77 us  [the longest x1 7.1 us: shards(): query_tensor = whole.reshape(qtok, heads_kv, query_group, head_dim)]
  transfers between devices with their start and end apart: 4 -> 18, of which waited for: 4 -> 15; matrix products, arithmetic and copies ran while one was open for 4% -> 7% of each run, Pallas kernels for 0% -> 0%
where the time goes in v1:
time: 551 us; the launch traced here: 548 us
  waiting for transfers between devices  230 us (42%)
  local copies, waits for them, and re-layouts  122 us (22%)
  blocking collectives  70.2 us (13%)
  matrix products  64.9 us (12%)
  starting transfers between devices  32.9 us (6%)
  other arithmetic  14.4 us (3%)
  between operations  13.2 us (2%)
    reduce_scatter x1, waiting for transfers between devices, shards(): lax.psum_scatter(numer, 'ctx', scatter_dimension=0, tiled=True)  81.4 us
    reduce_scatter x1, waiting for transfers between devices, shards(): lax.psum_scatter(jnp.dot(attn_cols, out_weight, preferred_element_type=jn...  76.6 us
    pmax x1, blocking collectives, shards(): row_max = lax.pmax(maxima, 'ctx')  57.8 us
    dot_general x16, matrix products, head_scores(): jnp.einsum('qge,ke->gqk', q_h, k_h, preferred_element_type=jnp.float32)  47.6 us
    reduce_scatter x1, waiting for transfers between devices, shards(): lax.psum_scatter(denom, 'ctx', scatter_dimension=0, tiled=True)  46.9 us
    ppermute x7, starting transfers between devices, ring_gather(): upper.append(lax.ppermute(upper[-1] if upper else x, axis, back))  32.4 us
    unnamed x44, local copies, waits for them, and re-layouts  30.2 us
    ppermute x8, waiting for transfers between devices, ring_gather(): lower.append(lax.ppermute(lower[-1] if lower else x, axis, pairs))  22.1 us
  transfers between devices with their start and end apart: 18, of which 15 were waited for; matrix products, arithmetic and copies ran while one was open for 7% of the time, Pallas kernels for 0%

profile of v1, /device:TPU:0, one launch (start us, length us, event | category | flops | bytes accessed | tf_op | source)
XLA Modules:
  0.0 547.9 jit_solution(13209127932098652076)
XLA Ops:
  7.0 8.2 %collective-permute-done = bf16[16,5120]{1,0:T(8,128)(2,1)S(1)} collective-permute-done((bf16[16,5120]{1,0:T(8,128)(2,1)}, bf16[16,5120]{1,0:T(8,128)(2,1)S(1)}, u32[]{:S(2)}, u32[]{:S(2)}) %collective-permute-start) | collective-permute-done | bytes 163872 | tf_op jit(solution)/shard_map/ppermute | solution.py:24
  15.2 4.4 collective-permute-start.8
  19.6 3.0 collective-permute-done.1
  23.4 4.6 collective-permute-start.9
  30.9 4.6 collective-permute-start.10
  35.5 2.2 collective-permute-done.3
  38.3 4.7 collective-permute-start.11
  43.0 2.2 collective-permute-done.4
  45.9 4.8 collective-permute-start.12
  50.7 2.2 collective-permute-done.5
  53.8 4.7 collective-permute-start.13
  60.7 4.7 copy.36
  65.4 4.7 copy.39
  70.1 4.7 copy.35
  74.9 4.5 collective-permute-start.14
  99.4 3.9 gather_fusion
  103.3 7.1 %reshape_reshape.3 = bf16[256,8,5,128]{3,2,1,0:T(8,128)(2,1)} reshape(bf16[16,16,5120]{2,1,0:T(8,128)(2,1)} %gather_fusion) | data formatting | bytes 5242880 | tf_op jit(solution)/shard_map/reshape;reshape | solution.py:41
  110.4 5.6 %copy.40 = bf16[256,8,5,128]{3,0,2,1:T(8,128)(2,1)} copy(bf16[256,8,5,128]{3,2,1,0:T(8,128)(2,1)} %reshape_reshape.3) | data formatting | bytes 5242880 | tf_op jit(solution)/shard_map/while | solution.py:87
  116.0 53.3 %while.28 = (s32[]{:T(128)}, f32[256,8,5]{0,2,1:T(8,128)S(1)}, s32[8,2,12]{2,1,0:T(2,128)}, bf16[1536,8,128]{2,0,1:T(8,128)(2,1)}, bf16[256,8,5,128]{3,0,2,1:T(8,128)(2,1)}, /*index=5*/s32[]{:T(128)}) while((s32[]{:T(128)}, f32[256,8,5]{0,2,1:T(8,128)S(1)}, s32[8,2,12]{2,1,0:T(2,128)}, bf16[1536,8,128]{2,0,1:T(8,128)(2,1)}, ...), condition=%wide.region_2.3_spmd, body=%wide.region_0.2_spmd.sunk | while | flops 509213472 | bytes 3102949 | solution.py:66
  117.9 2.2 copy.60
  120.2 2.5 fusion.33
  126.8 2.5 fusion.33
  133.5 2.5 fusion.33
  137.9 2.2 copy.60
  140.1 2.5 fusion.33
  146.8 2.5 fusion.33
  151.2 2.2 copy.60
  153.5 2.5 fusion.33
  160.1 2.5 fusion.33
  166.8 2.5 fusion.33
  169.3 57.8 %pmax.7 = f32[256,8,5]{0,2,1:T(8,128)S(1)} all-reduce(f32[256,8,5]{0,2,1:T(8,128)S(1)} %get-tuple-element.239), channel_id=1, replica_groups=mesh['groups'=2,'ctx'=16] {'ctx'}, use_global_device_ids=true, to_apply=%region_3.4 | all-reduce | flops 10240 | bytes 81920 | tf_op jit(solution)/shard_map/pmax | solution.py:69
  227.2 80.8 %while.29 = (s32[]{:T(128)}, f32[256,8,640]{0,2,1:T(8,128)}, f32[256,8,5]{0,2,1:T(8,128)S(1)}, bf16[1536,8,128]{0,2,1:T(8,128)(2,1)}, s32[8,2,12]{2,1,0:T(2,128)...) while((s32[]{:T(128)}, f32[256,8,640]{0,2,1:T(8,128)}, ...), condition=%wide.region_6.7_spmd, body=%wide.region_4.6_spmd.sunk | while | flops 1018428160 | bytes 13341961 | solution.py:87
  231.3 3.4 convert_reduce_fusion.2
  239.2 2.2 copy.62
  241.4 3.4 convert_reduce_fusion.2
  249.3 2.2 copy.62
  251.5 3.4 convert_reduce_fusion.2
  261.6 3.4 convert_reduce_fusion.2
  271.7 3.4 convert_reduce_fusion.2
  281.8 3.4 convert_reduce_fusion.2
  291.9 3.4 convert_reduce_fusion.2
  302.0 3.4 convert_reduce_fusion.2
  308.8 6.0 %copy.41 = f32[256,5120]{1,0:T(8,128)} copy(f32[256,5120]{0,1:T(8,128)} %bitcast.155) | data formatting | bytes 10485760 | tf_op jit(solution)/shard_map/reshape | solution.py:88
  314.9 46.9 %reduce-scatter.10.cloned.1.call-done = f32[16,40]{1,0:T(8,128)} async-done(((f32[256,40]{1,0:T(8,128)}), f32[16,40]{1,0:T(8,128)}) %reduce-scatter.10.cloned.1.call-update) | async-done | bytes 2576 | tf_op jit(solution)/shard_map/reduce_scatter | solution.py:92
  361.7 81.4 %reduce-scatter.6.cloned.1.call-done = f32[16,5120]{1,0:T(8,128)} async-done(((f32[256,5120]{1,0:T(8,128)}), f32[16,5120]{1,0:T(8,128)}) %reduce-scatter.6.cloned.1.call-update) | async-done | bytes 327696 | tf_op jit(solution)/shard_map/reduce_scatter | solution.py:91
  446.9 12.4 %all_to_all.19 = bf16[16,16,320]{2,0,1:T(8,128)(2,1)S(1)} all-to-all(bf16[16,16,320]{2,0,1:T(8,128)(2,1)S(1)} %copy.43), channel_id=1, replica_groups=mesh['groups'=2,'ctx'=16] {'ctx'}, dimensions={1} | all-to-all | bytes 327680 | tf_op jit(solution)/shard_map/all_to_all | solution.py:98
  459.2 3.9 fusion.21
  463.1 76.6 %reduce-scatter.8.cloned.1.call-done = f32[16,5120]{1,0:T(8,128)} async-done(((f32[256,5120]{1,0:T(8,128)}), f32[16,5120]{1,0:T(8,128)}) %reduce-scatter.8.cloned.1.call-update) | async-done | bytes 327696 | tf_op jit(solution)/shard_map/reduce_scatter | solution.py:101
  (177 shorter events, 109.5 us)
Async XLA Ops:
  6.5 452.7 %copy-start = (bf16[320,5120]{1,0:T(8,128)(2,1)S(1)}, bf16[320,5120]{1,0:T(8,128)(2,1)}, u32[]{:S(2)}) copy-start(bf16[320,5120]{1,0:T(8,128)(2,1)} %param.13) | copy-start | bytes 9830404
  6.5 355.2 %reduce-scatter.10.cloned.1.call-start = ((), (), s32[]{:S(2)}) async-start(), calls=%async_computation.6 | async-start | bytes 139264 | tf_op jit(solution)/shard_map/reduce_scatter | solution.py:92
  6.5 8.6 %collective-permute-start = (bf16[16,5120]{1,0:T(8,128)(2,1)}, bf16[16,5120]{1,0:T(8,128)(2,1)S(1)}, u32[]{:S(2)}, u32[]{:S(2)}) collective-permute-start(bf16[16,5120]{1,0:T(8,128)(2,1)} %param.9), channel_id=1, source_target_pairs={{0,1},{1,2},{2,3},{3,4},{4,5},{5,6},{6,7},{7,8},{8,9},{9,10},{10,1... | collective-permute-start | bytes 491528 | tf_op jit(solution)/shard_map/ppermute | solution.py:24
  15.2 7.4 %collective-permute-start.1 = (bf16[16,5120]{1,0:T(8,128)(2,1)S(1)}, bf16[16,5120]{1,0:T(8,128)(2,1)S(1)}, u32[]{:S(2)}, u32[]{:S(2)}) collective-permute-start(bf16[16,5120]{1,0:T(8,128)(2,1)S(1)} %collective-permute-done), channel_id=1, source_target_pairs={{0,1},{1,2},{2,3},{3,4},{4,5},{5,6},{6,7},{7,8},{8,9},{9,10},{10,1... | collective-permute-start | bytes 491528 | tf_op jit(solution)/shard_map/ppermute | solution.py:24
  15.2 7.6 %collective-permute-start.8 = (bf16[16,5120]{1,0:T(8,128)(2,1)}, bf16[16,5120]{1,0:T(8,128)(2,1)S(1)}, u32[]{:S(2)}, u32[]{:S(2)}) collective-permute-start(bf16[16,5120]{1,0:T(8,128)(2,1)} %param.9), channel_id=1, source_target_pairs={{1,0},{2,1},{3,2},{4,3},{5,4},{6,5},{7,6},{8,7},{9,8},{10,9},{11,1... | collective-permute-start | bytes 491528 | tf_op jit(solution)/shard_map/ppermute | solution.py:26
  22.6 8.3 %copy-start.4 = (bf16[16,5120]{1,0:T(8,128)(2,1)}, bf16[16,5120]{1,0:T(8,128)(2,1)S(1)}, u32[]{:S(2)}) copy-start(bf16[16,5120]{1,0:T(8,128)(2,1)S(1)} %collective-permute-done.1) | copy-start | bytes 491524
  22.6 7.6 %collective-permute-start.2 = (bf16[16,5120]{1,0:T(8,128)(2,1)S(1)}, bf16[16,5120]{1,0:T(8,128)(2,1)S(1)}, u32[]{:S(2)}, u32[]{:S(2)}) collective-permute-start(bf16[16,5120]{1,0:T(8,128)(2,1)S(1)} %collective-permute-done.1), channel_id=1, source_target_pairs={{0,1},{1,2},{2,3},{3,4},{4,5},{5,6},{6,7},{7,8},{8,9},{9,10},{10,1... | collective-permute-start | bytes 491528 | tf_op jit(solution)/shard_map/ppermute | solution.py:24
  22.8 0.7 copy-start.2
  23.4 7.4 %collective-permute-start.9 = (bf16[16,5120]{1,0:T(8,128)(2,1)S(1)}, bf16[16,5120]{1,0:T(8,128)(2,1)S(1)}, u32[]{:S(2)}, u32[]{:S(2)}) collective-permute-start(bf16[16,5120]{1,0:T(8,128)(2,1)S(1)} %collective-permute-done.8), channel_id=1, source_target_pairs={{1,0},{2,1},{3,2},{4,3},{5,4},{6,5},{7,6},{8,7},{9,8},{10,9},{11,1... | collective-permute-start | bytes 491528 | tf_op jit(solution)/shard_map/ppermute | solution.py:26
  30.2 8.2 %copy-start.7 = (bf16[16,5120]{1,0:T(8,128)(2,1)}, bf16[16,5120]{1,0:T(8,128)(2,1)S(1)}, u32[]{:S(2)}) copy-start(bf16[16,5120]{1,0:T(8,128)(2,1)S(1)} %collective-permute-done.2) | copy-start | bytes 491524
  30.2 7.6 %collective-permute-start.3 = (bf16[16,5120]{1,0:T(8,128)(2,1)S(1)}, bf16[16,5120]{1,0:T(8,128)(2,1)S(1)}, u32[]{:S(2)}, u32[]{:S(2)}) collective-permute-start(bf16[16,5120]{1,0:T(8,128)(2,1)S(1)} %collective-permute-done.2), channel_id=1, source_target_pairs={{0,1},{1,2},{2,3},{3,4},{4,5},{5,6},{6,7},{7,8},{8,9},{9,10},{10,1... | collective-permute-start | bytes 491528 | tf_op jit(solution)/shard_map/ppermute | solution.py:24
  30.9 4.6 copy-start.5
  30.9 7.4 %collective-permute-start.10 = (bf16[16,5120]{1,0:T(8,128)(2,1)S(1)}, bf16[16,5120]{1,0:T(8,128)(2,1)S(1)}, u32[]{:S(2)}, u32[]{:S(2)}) collective-permute-start(bf16[16,5120]{1,0:T(8,128)(2,1)S(1)} %collective-permute-done.9), channel_id=1, source_target_pairs={{1,0},{2,1},{3,2},{4,3},{5,4},{6,5},{7,6},{8,7},{9,8},{10,9},{11,1... | collective-permute-start | bytes 491528 | tf_op jit(solution)/shard_map/ppermute | solution.py:26
  37.7 8.2 %copy-start.10 = (bf16[16,5120]{1,0:T(8,128)(2,1)}, bf16[16,5120]{1,0:T(8,128)(2,1)S(1)}, u32[]{:S(2)}) copy-start(bf16[16,5120]{1,0:T(8,128)(2,1)S(1)} %collective-permute-done.3) | copy-start | bytes 491524
  37.7 7.5 %collective-permute-start.4 = (bf16[16,5120]{1,0:T(8,128)(2,1)S(1)}, bf16[16,5120]{1,0:T(8,128)(2,1)S(1)}, u32[]{:S(2)}, u32[]{:S(2)}) collective-permute-start(bf16[16,5120]{1,0:T(8,128)(2,1)S(1)} %collective-permute-done.3), channel_id=1, source_target_pairs={{0,1},{1,2},{2,3},{3,4},{4,5},{5,6},{6,7},{7,8},{8,9},{9,10},{10,1... | collective-permute-start | bytes 491528 | tf_op jit(solution)/shard_map/ppermute | solution.py:24
  38.3 4.7 copy-start.8
  38.3 7.5 %collective-permute-start.11 = (bf16[16,5120]{1,0:T(8,128)(2,1)S(1)}, bf16[16,5120]{1,0:T(8,128)(2,1)}, u32[]{:S(2)}, u32[]{:S(2)}) collective-permute-start(bf16[16,5120]{1,0:T(8,128)(2,1)S(1)} %collective-permute-done.10), channel_id=1, source_target_pairs={{1,0},{2,1},{3,2},{4,3},{5,4},{6,5},{7,6},{8,7},{9,8},{10,9},{11,1... | collective-permute-start | bytes 491528 | tf_op jit(solution)/shard_map/ppermute | solution.py:26
  45.3 5.4 copy-start.11
  45.3 7.7 %collective-permute-start.5 = (bf16[16,5120]{1,0:T(8,128)(2,1)S(1)}, bf16[16,5120]{1,0:T(8,128)(2,1)}, u32[]{:S(2)}, u32[]{:S(2)}) collective-permute-start(bf16[16,5120]{1,0:T(8,128)(2,1)S(1)} %collective-permute-done.4), channel_id=1, source_target_pairs={{0,1},{1,2},{2,3},{3,4},{4,5},{5,6},{6,7},{7,8},{8,9},{9,10},{10,1... | collective-permute-start | bytes 491528 | tf_op jit(solution)/shard_map/ppermute | solution.py:24
  45.9 8.0 %collective-permute-start.12 = (bf16[16,5120]{1,0:T(8,128)(2,1)}, bf16[16,5120]{1,0:T(8,128)(2,1)}, u32[]{:S(2)}, u32[]{:S(2)}) collective-permute-start(bf16[16,5120]{1,0:T(8,128)(2,1)} %collective-permute-done.11), channel_id=1, source_target_pairs={{1,0},{2,1},{3,2},{4,3},{5,4},{6,5},{7,6},{8,7},{9,8},{10,9},{11,1... | collective-permute-start | bytes 491528 | tf_op jit(solution)/shard_map/ppermute | solution.py:26
  52.9 7.8 %collective-permute-start.6 = (bf16[16,5120]{1,0:T(8,128)(2,1)}, bf16[16,5120]{1,0:T(8,128)(2,1)}, u32[]{:S(2)}, u32[]{:S(2)}) collective-permute-start(bf16[16,5120]{1,0:T(8,128)(2,1)} %collective-permute-done.5), channel_id=1, source_target_pairs={{0,1},{1,2},{2,3},{3,4},{4,5},{5,6},{6,7},{7,8},{8,9},{9,10},{10,1... | collective-permute-start | bytes 491528 | tf_op jit(solution)/shard_map/ppermute | solution.py:24
  53.8 21.0 %collective-permute-start.13 = (bf16[16,5120]{1,0:T(8,128)(2,1)}, bf16[16,5120]{1,0:T(8,128)(2,1)}, u32[]{:S(2)}, u32[]{:S(2)}) collective-permute-start(bf16[16,5120]{1,0:T(8,128)(2,1)} %collective-permute-done.12), channel_id=1, source_target_pairs={{1,0},{2,1},{3,2},{4,3},{5,4},{6,5},{7,6},{8,7},{9,8},{10,9},{11,1... | collective-permute-start | bytes 491528 | tf_op jit(solution)/shard_map/ppermute | solution.py:26
  60.7 18.7 %collective-permute-start.7 = (bf16[16,5120]{1,0:T(8,128)(2,1)}, bf16[16,5120]{1,0:T(8,128)(2,1)}, u32[]{:S(2)}, u32[]{:S(2)}) collective-permute-start(bf16[16,5120]{1,0:T(8,128)(2,1)} %collective-permute-done.6), channel_id=1, source_target_pairs={{0,1},{1,2},{2,3},{3,4},{4,5},{5,6},{6,7},{7,8},{8,9},{9,10},{10,1... | collective-permute-start | bytes 491528 | tf_op jit(solution)/shard_map/ppermute | solution.py:24
  74.8 16.4 %copy-start.1 = (bf16[16,5120]{1,0:T(8,128)(2,1)S(1)}, bf16[16,5120]{1,0:T(8,128)(2,1)}, u32[]{:S(2)}) copy-start(bf16[16,5120]{1,0:T(8,128)(2,1)} %param.9) | copy-start | bytes 491524
  74.8 17.1 %copy-start.3 = (bf16[16,5120]{1,0:T(8,128)(2,1)S(1)}, bf16[16,5120]{1,0:T(8,128)(2,1)}, u32[]{:S(2)}) copy-start(bf16[16,5120]{1,0:T(8,128)(2,1)} %copy-done.2) | copy-start | bytes 491524
  74.8 17.7 %copy-start.6 = (bf16[16,5120]{1,0:T(8,128)(2,1)S(1)}, bf16[16,5120]{1,0:T(8,128)(2,1)}, u32[]{:S(2)}) copy-start(bf16[16,5120]{1,0:T(8,128)(2,1)} %copy-done.5) | copy-start | bytes 491524
  74.8 18.4 %copy-start.9 = (bf16[16,5120]{1,0:T(8,128)(2,1)S(1)}, bf16[16,5120]{1,0:T(8,128)(2,1)}, u32[]{:S(2)}) copy-start(bf16[16,5120]{1,0:T(8,128)(2,1)} %copy-done.8) | copy-start | bytes 491524
  74.9 23.8 %collective-permute-start.14 = (bf16[16,5120]{1,0:T(8,128)(2,1)}, bf16[16,5120]{1,0:T(8,128)(2,1)S(1)}, u32[]{:S(2)}, u32[]{:S(2)}) collective-permute-start(bf16[16,5120]{1,0:T(8,128)(2,1)} %collective-permute-done.13), channel_id=1, source_target_pairs={{1,0},{2,1},{3,2},{4,3},{5,4},{6,5},{7,6},{8,7},{9,8},{10,9},{11,1... | collective-permute-start | bytes 491528 | tf_op jit(solution)/shard_map/ppermute | solution.py:26
  116.0 111.2 %copy-start.12 = (f32[256,8,5]{0,2,1:T(8,128)S(1)}, f32[256,8,5]{0,2,1:T(8,128)}, u32[]{:S(2)}) copy-start(f32[256,8,5]{0,2,1:T(8,128)} %custom-call.5) | copy-start | bytes 122884
  308.8 134.4 %reduce-scatter.6.cloned.1.call-start = ((), (), s32[]{:S(2)}) async-start(), calls=%async_computation.4 | async-start | bytes 5570560 | tf_op jit(solution)/shard_map/reduce_scatter | solution.py:91
  314.8 224.9 %reduce-scatter.8.cloned.1.call-start = ((), (), s32[]{:S(2)}) async-start(), calls=%async_computation.5 | async-start | bytes 5570560 | tf_op jit(solution)/shard_map/reduce_scatter | solution.py:101
Sparse Core Ops, SparseCore 0:
  308.9 52.7 reduce-scatter.9
  365.6 77.5 reduce-scatter.5
  463.3 76.4 reduce-scatter.7
